TPU v7x, 128 devices: a whole 4x4x4 slice. The times are simulated.
128 devices in a mesh: section: 8 (over x, core), tp: 16 (over z, y).
Axes of the slice: x: 4, y: 4, z: 4, core: 2. Of those that a mesh axis runs over, the one named last changes fastest.
Arguments:
- layer_inputs: bfloat16 [16, 512, 4096], P('section', None, 'tp'), may hold values from -6 to 6
- weights: bfloat16 [16, 4096, 4096], P('section', 'tp'), may hold values from -0.046875 to 0.046875
- input_basis: bfloat16 [16, 4096, 64], P('section', 'tp'), may hold values from -0.09375 to 0.09375
- output_basis: bfloat16 [16, 4096, 32], P('section', 'tp'), may hold values from -0.09375 to 0.09375
- queries: bfloat16 [16, 512, 2048], P('section', 'tp'), may hold values from -0.00390625 to 0.00390625
- top_cotangent: bfloat16 [512, 4096], replicated, may hold values from -6 to 6
- sequence_example: int32 [4], replicated, may hold values from 0 to 1
Outputs:
- scores: float32 [2, 512], P(None, 'tp')
All inputs are finite; a program needn't handle non-finite values.
Results may differ from a plain program's by a relative error of at most 0.0094.
Values may be sent and summed in bfloat16 or wider, within the bound.
No kernel may reach another device: no remote copies, remote signals or barrier semaphores. Data moves between devices by JAX's collectives and lax.ppermute only.
A program may use at most 64 MiB of HBM per device.

v0:
```python
import jax
import jax.numpy as jnp
from jax import lax
from jax.sharding import PartitionSpec as P

SEQLEN = 128
SEQ_MB = 1
MB = 4
EXAMPLES = 2


def from_behind(value, axis, by):
    size = lax.axis_size(axis)
    pairs = [(i, i + by) for i in range(size) if 0 <= i + by < size]
    return lax.ppermute(value, axis, pairs)


def silu_parts(values):
    floats = values.astype(jnp.float32)
    logistic = jax.nn.sigmoid(floats)
    return ((floats * logistic).astype(jnp.bfloat16), logistic * (1.0 + floats * (1.0 - logistic)))


def contract_columns(portion, matrix):
    return lax.dot_general(
        portion, matrix, (((1,), (1,)), ((), ())), preferred_element_type=jnp.float32
    )


def outer_rows(out_feats, in_feats):
    joined = out_feats[:, :, :, None] * in_feats[:, :, None, :]
    return joined.reshape(joined.shape[0], joined.shape[1], -1)


def shards(
    layer_inputs, weights, input_basis, output_basis, queries, top_cotangent, sequence_example
):
    section_count = lax.axis_size("section")
    section_rank = lax.axis_index("section")
    tp_rank = lax.axis_index("tp")
    width_local = layer_inputs.shape[2]
    width_full = weights.shape[2]
    total_tokens = layer_inputs.shape[1]
    block_rows = SEQ_MB * SEQLEN
    activated, slopes = silu_parts(layer_inputs)
    partial_in = jnp.einsum(
        "ltd,ldr->tlr", activated, input_basis, preferred_element_type=jnp.float32
    )
    in_feats = lax.psum(partial_in.reshape(total_tokens, -1), "tp").reshape(partial_in.shape)
    example_index = jnp.arange(EXAMPLES, dtype=jnp.int32)
    is_top = section_rank == section_count - 1

    def fold_lower(portion):
        return contract_columns(portion, weights[0])

    def tick(tick_index, state):
        outgoing, grads, stored = state
        micro_index = tick_index - (section_count - 1 - section_rank)
        valid = (micro_index >= 0) & (micro_index < MB)
        micro_clip = jnp.clip(micro_index, 0, MB - 1)
        first_row = micro_clip * block_rows
        slope_block = lax.dynamic_slice_in_dim(slopes, first_row, block_rows, 1)
        received = from_behind(outgoing, "section", -1)
        top_block = lax.dynamic_slice_in_dim(top_cotangent, first_row, block_rows, 0)
        upper_full = jnp.where(is_top, top_block, received)
        upper_own = lax.dynamic_slice_in_dim(upper_full, tp_rank * width_local, width_local, 1)
        upper_branch = lax.dot_general(
            upper_full, weights[1], (((1,), (1,)), ((), ())), preferred_element_type=jnp.float32
        )
        middle_own = (upper_own.astype(jnp.float32) + slope_block[1] * upper_branch).astype(
            jnp.bfloat16
        )
        lower_branch = fold_lower(lax.all_gather(middle_own, "tp", axis=1, tiled=True))
        lower_own = (middle_own.astype(jnp.float32) + slope_block[0] * lower_branch).astype(
            jnp.bfloat16
        )
        new_outgoing = lax.all_gather(lower_own, "tp", axis=1, tiled=True)
        cotangents = jnp.stack([middle_own, upper_own], 0)
        partial_out = jnp.einsum(
            "lrd,ldk->rlk", cotangents, output_basis, preferred_element_type=jnp.float32
        )
        out_feats = lax.psum(partial_out.reshape(block_rows, -1), "tp").reshape(partial_out.shape)
        in_block = lax.dynamic_slice_in_dim(in_feats, first_row, block_rows, 0)
        block_examples = jnp.repeat(
            lax.dynamic_slice_in_dim(sequence_example, micro_clip * SEQ_MB, SEQ_MB, 0), SEQLEN
        )
        selector = (example_index[:, None] == block_examples[None, :]).astype(
            jnp.float32
        ) * valid.astype(jnp.float32)
        grads = grads + jnp.einsum(
            "er,rlk->lek",
            selector,
            outer_rows(out_feats, in_block),
            precision=lax.Precision.HIGHEST,
        )
        return (new_outgoing, grads, stored)

    outgoing_init = jnp.zeros((block_rows, width_full), jnp.bfloat16)
    grads_init = jnp.zeros((2, EXAMPLES, queries.shape[2]), jnp.float32)
    stored_init = jnp.zeros((1,), jnp.bfloat16)
    final_out, grads, stored = lax.fori_loop(
        0, MB + section_count - 1, tick, (outgoing_init, grads_init, stored_init)
    )
    layer_scores = jnp.einsum(
        "lek,lqk->eq", grads, queries.astype(jnp.float32), precision=lax.Precision.HIGHEST
    )
    return lax.psum(layer_scores, "section")


def solution(mesh):
    placed = (
        P("section", None, "tp"),
        P("section", "tp", None),
        P("section", "tp", None),
        P("section", "tp", None),
        P("section", "tp", None),
        P(),
        P(),
    )
    return jax.shard_map(
        shards, mesh=mesh, in_specs=placed, out_specs=P(None, "tp"), check_vma=False
    )
```

profile of v0, /device:TPU:1, one launch (start us, length us, event | category | flops | bytes accessed | tf_op | source)
XLA Modules:
  0.0 1662.4 jit_solution(13824720775074881913)
XLA Ops:
  9.2 87.7 %all-reduce.2.cloned.1.call-done = f32[512,2,64]{0,2,1:T(8,128)} async-done(((f32[512,2,64]{0,2,1:T(8,128)}), f32[512,2,64]{0,2,1:T(8,128)}) %all-reduce.2.cloned.1.call-update) | async-done | bytes 262160 | tf_op jit(solution)/shard_map/psum | solution.py:49
  98.0 1529.4 %while.18 = (s32[]{:T(128)}, bf16[128,4096]{1,0:T(8,128)(2,1)}, f32[2,2,2048]{2,1,0:T(2,128)S(1)}, pred[]{:T(512)}, s32[]{:T(128)}, /*index=5*/bf16[512,4096]{1,...) while((s32[]{:T(128)}, bf16[128,4096]{1,0:T(8,128)(2,1)}, ...), condition=%wide.region_3.4_spmd.clone, body=%wide.region_1.3_spmd.clone.sunk | while | flops 555048960 | bytes 25986044 | solution.py:101
  98.0 3.9 collective-permute-start
  101.9 13.7 collective-permute-done
  120.3 40.6 %all-gather.3.cloned.1.call-done = bf16[128,4096]{1,0:T(8,128)(2,1)} async-done(((bf16[128,256]{1,0:T(8,128)(2,1)}), bf16[128,4096]{1,0:T(8,128)(2,1)}) %all-gather.3.cloned.1.call-update) | async-done | bytes 1048592 | tf_op jit(solution)/shard_map/while/body/eval_jaxpr/all_gather | solution.py:73
  160.9 3.3 add_convert_fusion.5
  166.6 58.4 %psum.31 = f32[128,2,32]{0,2,1:T(8,128)S(1)} all-reduce(f32[128,2,32]{0,2,1:T(8,128)S(1)} %convolution_bitcast_fusion.5), channel_id=1, replica_groups=mesh['section'=8,'tp'=16] {'tp'}, use_global_device_ids=true, to_apply=%region_2.2 | all-reduce | flops 8192 | bytes 65536 | tf_op jit(solution)/shard_map/while/body/eval_jaxpr/psum | solution.py:82
  227.2 17.7 %collective-permute-start = (bf16[128,4096]{1,0:T(8,128)(2,1)}, bf16[128,4096]{1,0:T(8,128)(2,1)S(1)}, u32[]{:S(2)}, u32[]{:S(2)}) collective-permute-start(bf16[128,4096]{1,0:T(8,128)(2,1)} %get-tuple-element.465), channel_id=1, source_target_pairs={{16,0},{32,16},{48,32},{64,48},{80,64},{96,80},{112,96},{17,1},{33... | collective-permute-start | bytes 3145736 | tf_op jit(solution)/shard_map/while/body/eval_jaxpr/ppermute | solution.py:15
  244.9 13.7 collective-permute-done
  260.2 3.1 add_convert_fusion.4
  263.3 37.6 %all-gather.3.cloned.1.call-done = bf16[128,4096]{1,0:T(8,128)(2,1)} async-done(((bf16[128,256]{1,0:T(8,128)(2,1)}), bf16[128,4096]{1,0:T(8,128)(2,1)}) %all-gather.3.cloned.1.call-update) | async-done | bytes 1048592 | tf_op jit(solution)/shard_map/while/body/eval_jaxpr/all_gather | solution.py:73
  300.9 3.3 add_convert_fusion.5
  306.6 58.4 %psum.31 = f32[128,2,32]{0,2,1:T(8,128)S(1)} all-reduce(f32[128,2,32]{0,2,1:T(8,128)S(1)} %convolution_bitcast_fusion.5), channel_id=1, replica_groups=mesh['section'=8,'tp'=16] {'tp'}, use_global_device_ids=true, to_apply=%region_2.2 | all-reduce | flops 8192 | bytes 65536 | tf_op jit(solution)/shard_map/while/body/eval_jaxpr/psum | solution.py:82
  367.3 17.7 %collective-permute-start = (bf16[128,4096]{1,0:T(8,128)(2,1)}, bf16[128,4096]{1,0:T(8,128)(2,1)S(1)}, u32[]{:S(2)}, u32[]{:S(2)}) collective-permute-start(bf16[128,4096]{1,0:T(8,128)(2,1)} %get-tuple-element.465), channel_id=1, source_target_pairs={{16,0},{32,16},{48,32},{64,48},{80,64},{96,80},{112,96},{17,1},{33... | collective-permute-start | bytes 3145736 | tf_op jit(solution)/shard_map/while/body/eval_jaxpr/ppermute | solution.py:15
  385.0 13.7 collective-permute-done
  400.2 3.1 add_convert_fusion.4
  403.3 37.6 %all-gather.3.cloned.1.call-done = bf16[128,4096]{1,0:T(8,128)(2,1)} async-done(((bf16[128,256]{1,0:T(8,128)(2,1)}), bf16[128,4096]{1,0:T(8,128)(2,1)}) %all-gather.3.cloned.1.call-update) | async-done | bytes 1048592 | tf_op jit(solution)/shard_map/while/body/eval_jaxpr/all_gather | solution.py:73
  441.0 3.3 add_convert_fusion.5
  446.6 58.4 %psum.31 = f32[128,2,32]{0,2,1:T(8,128)S(1)} all-reduce(f32[128,2,32]{0,2,1:T(8,128)S(1)} %convolution_bitcast_fusion.5), channel_id=1, replica_groups=mesh['section'=8,'tp'=16] {'tp'}, use_global_device_ids=true, to_apply=%region_2.2 | all-reduce | flops 8192 | bytes 65536 | tf_op jit(solution)/shard_map/while/body/eval_jaxpr/psum | solution.py:82
  507.3 17.7 %collective-permute-start = (bf16[128,4096]{1,0:T(8,128)(2,1)}, bf16[128,4096]{1,0:T(8,128)(2,1)S(1)}, u32[]{:S(2)}, u32[]{:S(2)}) collective-permute-start(bf16[128,4096]{1,0:T(8,128)(2,1)} %get-tuple-element.465), channel_id=1, source_target_pairs={{16,0},{32,16},{48,32},{64,48},{80,64},{96,80},{112,96},{17,1},{33... | collective-permute-start | bytes 3145736 | tf_op jit(solution)/shard_map/while/body/eval_jaxpr/ppermute | solution.py:15
  525.0 13.7 collective-permute-done
  540.2 3.1 add_convert_fusion.4
  543.4 37.6 %all-gather.3.cloned.1.call-done = bf16[128,4096]{1,0:T(8,128)(2,1)} async-done(((bf16[128,256]{1,0:T(8,128)(2,1)}), bf16[128,4096]{1,0:T(8,128)(2,1)}) %all-gather.3.cloned.1.call-update) | async-done | bytes 1048592 | tf_op jit(solution)/shard_map/while/body/eval_jaxpr/all_gather | solution.py:73
  581.0 3.3 add_convert_fusion.5
  586.7 58.4 %psum.31 = f32[128,2,32]{0,2,1:T(8,128)S(1)} all-reduce(f32[128,2,32]{0,2,1:T(8,128)S(1)} %convolution_bitcast_fusion.5), channel_id=1, replica_groups=mesh['section'=8,'tp'=16] {'tp'}, use_global_device_ids=true, to_apply=%region_2.2 | all-reduce | flops 8192 | bytes 65536 | tf_op jit(solution)/shard_map/while/body/eval_jaxpr/psum | solution.py:82
  647.3 17.7 %collective-permute-start = (bf16[128,4096]{1,0:T(8,128)(2,1)}, bf16[128,4096]{1,0:T(8,128)(2,1)S(1)}, u32[]{:S(2)}, u32[]{:S(2)}) collective-permute-start(bf16[128,4096]{1,0:T(8,128)(2,1)} %get-tuple-element.465), channel_id=1, source_target_pairs={{16,0},{32,16},{48,32},{64,48},{80,64},{96,80},{112,96},{17,1},{33... | collective-permute-start | bytes 3145736 | tf_op jit(solution)/shard_map/while/body/eval_jaxpr/ppermute | solution.py:15
  665.0 13.7 collective-permute-done
  683.4 37.6 %all-gather.3.cloned.1.call-done = bf16[128,4096]{1,0:T(8,128)(2,1)} async-done(((bf16[128,256]{1,0:T(8,128)(2,1)}), bf16[128,4096]{1,0:T(8,128)(2,1)}) %all-gather.3.cloned.1.call-update) | async-done | bytes 1048592 | tf_op jit(solution)/shard_map/while/body/eval_jaxpr/all_gather | solution.py:73
  721.0 3.3 add_convert_fusion.5
  726.7 58.4 %psum.31 = f32[128,2,32]{0,2,1:T(8,128)S(1)} all-reduce(f32[128,2,32]{0,2,1:T(8,128)S(1)} %convolution_bitcast_fusion.5), channel_id=1, replica_groups=mesh['section'=8,'tp'=16] {'tp'}, use_global_device_ids=true, to_apply=%region_2.2 | all-reduce | flops 8192 | bytes 65536 | tf_op jit(solution)/shard_map/while/body/eval_jaxpr/psum | solution.py:82
  787.3 17.7 %collective-permute-start = (bf16[128,4096]{1,0:T(8,128)(2,1)}, bf16[128,4096]{1,0:T(8,128)(2,1)S(1)}, u32[]{:S(2)}, u32[]{:S(2)}) collective-permute-start(bf16[128,4096]{1,0:T(8,128)(2,1)} %get-tuple-element.465), channel_id=1, source_target_pairs={{16,0},{32,16},{48,32},{64,48},{80,64},{96,80},{112,96},{17,1},{33... | collective-permute-start | bytes 3145736 | tf_op jit(solution)/shard_map/while/body/eval_jaxpr/ppermute | solution.py:15
  805.0 13.7 collective-permute-done
  823.4 37.6 %all-gather.3.cloned.1.call-done = bf16[128,4096]{1,0:T(8,128)(2,1)} async-done(((bf16[128,256]{1,0:T(8,128)(2,1)}), bf16[128,4096]{1,0:T(8,128)(2,1)}) %all-gather.3.cloned.1.call-update) | async-done | bytes 1048592 | tf_op jit(solution)/shard_map/while/body/eval_jaxpr/all_gather | solution.py:73
  861.1 3.3 add_convert_fusion.5
  866.7 58.4 %psum.31 = f32[128,2,32]{0,2,1:T(8,128)S(1)} all-reduce(f32[128,2,32]{0,2,1:T(8,128)S(1)} %convolution_bitcast_fusion.5), channel_id=1, replica_groups=mesh['section'=8,'tp'=16] {'tp'}, use_global_device_ids=true, to_apply=%region_2.2 | all-reduce | flops 8192 | bytes 65536 | tf_op jit(solution)/shard_map/while/body/eval_jaxpr/psum | solution.py:82
  927.4 17.7 %collective-permute-start = (bf16[128,4096]{1,0:T(8,128)(2,1)}, bf16[128,4096]{1,0:T(8,128)(2,1)S(1)}, u32[]{:S(2)}, u32[]{:S(2)}) collective-permute-start(bf16[128,4096]{1,0:T(8,128)(2,1)} %get-tuple-element.465), channel_id=1, source_target_pairs={{16,0},{32,16},{48,32},{64,48},{80,64},{96,80},{112,96},{17,1},{33... | collective-permute-start | bytes 3145736 | tf_op jit(solution)/shard_map/while/body/eval_jaxpr/ppermute | solution.py:15
  945.1 13.7 collective-permute-done
  960.3 3.1 add_convert_fusion.4
  963.4 37.6 %all-gather.3.cloned.1.call-done = bf16[128,4096]{1,0:T(8,128)(2,1)} async-done(((bf16[128,256]{1,0:T(8,128)(2,1)}), bf16[128,4096]{1,0:T(8,128)(2,1)}) %all-gather.3.cloned.1.call-update) | async-done | bytes 1048592 | tf_op jit(solution)/shard_map/while/body/eval_jaxpr/all_gather | solution.py:73
  1001.1 3.3 add_convert_fusion.5
  1006.7 58.4 %psum.31 = f32[128,2,32]{0,2,1:T(8,128)S(1)} all-reduce(f32[128,2,32]{0,2,1:T(8,128)S(1)} %convolution_bitcast_fusion.5), channel_id=1, replica_groups=mesh['section'=8,'tp'=16] {'tp'}, use_global_device_ids=true, to_apply=%region_2.2 | all-reduce | flops 8192 | bytes 65536 | tf_op jit(solution)/shard_map/while/body/eval_jaxpr/psum | solution.py:82
  1067.4 17.7 %collective-permute-start = (bf16[128,4096]{1,0:T(8,128)(2,1)}, bf16[128,4096]{1,0:T(8,128)(2,1)S(1)}, u32[]{:S(2)}, u32[]{:S(2)}) collective-permute-start(bf16[128,4096]{1,0:T(8,128)(2,1)} %get-tuple-element.465), channel_id=1, source_target_pairs={{16,0},{32,16},{48,32},{64,48},{80,64},{96,80},{112,96},{17,1},{33... | collective-permute-start | bytes 3145736 | tf_op jit(solution)/shard_map/while/body/eval_jaxpr/ppermute | solution.py:15
  1085.1 13.7 collective-permute-done
  1100.3 3.1 add_convert_fusion.4
  1103.5 37.6 %all-gather.3.cloned.1.call-done = bf16[128,4096]{1,0:T(8,128)(2,1)} async-done(((bf16[128,256]{1,0:T(8,128)(2,1)}), bf16[128,4096]{1,0:T(8,128)(2,1)}) %all-gather.3.cloned.1.call-update) | async-done | bytes 1048592 | tf_op jit(solution)/shard_map/while/body/eval_jaxpr/all_gather | solution.py:73
  1141.1 3.3 add_convert_fusion.5
  1146.8 58.4 %psum.31 = f32[128,2,32]{0,2,1:T(8,128)S(1)} all-reduce(f32[128,2,32]{0,2,1:T(8,128)S(1)} %convolution_bitcast_fusion.5), channel_id=1, replica_groups=mesh['section'=8,'tp'=16] {'tp'}, use_global_device_ids=true, to_apply=%region_2.2 | all-reduce | flops 8192 | bytes 65536 | tf_op jit(solution)/shard_map/while/body/eval_jaxpr/psum | solution.py:82
  1207.4 17.7 %collective-permute-start = (bf16[128,4096]{1,0:T(8,128)(2,1)}, bf16[128,4096]{1,0:T(8,128)(2,1)S(1)}, u32[]{:S(2)}, u32[]{:S(2)}) collective-permute-start(bf16[128,4096]{1,0:T(8,128)(2,1)} %get-tuple-element.465), channel_id=1, source_target_pairs={{16,0},{32,16},{48,32},{64,48},{80,64},{96,80},{112,96},{17,1},{33... | collective-permute-start | bytes 3145736 | tf_op jit(solution)/shard_map/while/body/eval_jaxpr/ppermute | solution.py:15
  1225.1 13.7 collective-permute-done
  1240.3 3.1 add_convert_fusion.4
  1243.5 37.6 %all-gather.3.cloned.1.call-done = bf16[128,4096]{1,0:T(8,128)(2,1)} async-done(((bf16[128,256]{1,0:T(8,128)(2,1)}), bf16[128,4096]{1,0:T(8,128)(2,1)}) %all-gather.3.cloned.1.call-update) | async-done | bytes 1048592 | tf_op jit(solution)/shard_map/while/body/eval_jaxpr/all_gather | solution.py:73
  1281.1 3.3 add_convert_fusion.5
  1286.8 58.4 %psum.31 = f32[128,2,32]{0,2,1:T(8,128)S(1)} all-reduce(f32[128,2,32]{0,2,1:T(8,128)S(1)} %convolution_bitcast_fusion.5), channel_id=1, replica_groups=mesh['section'=8,'tp'=16] {'tp'}, use_global_device_ids=true, to_apply=%region_2.2 | all-reduce | flops 8192 | bytes 65536 | tf_op jit(solution)/shard_map/while/body/eval_jaxpr/psum | solution.py:82
  1347.4 17.7 %collective-permute-start = (bf16[128,4096]{1,0:T(8,128)(2,1)}, bf16[128,4096]{1,0:T(8,128)(2,1)S(1)}, u32[]{:S(2)}, u32[]{:S(2)}) collective-permute-start(bf16[128,4096]{1,0:T(8,128)(2,1)} %get-tuple-element.465), channel_id=1, source_target_pairs={{16,0},{32,16},{48,32},{64,48},{80,64},{96,80},{112,96},{17,1},{33... | collective-permute-start | bytes 3145736 | tf_op jit(solution)/shard_map/while/body/eval_jaxpr/ppermute | solution.py:15
  1365.1 13.7 collective-permute-done
  1383.5 37.6 %all-gather.3.cloned.1.call-done = bf16[128,4096]{1,0:T(8,128)(2,1)} async-done(((bf16[128,256]{1,0:T(8,128)(2,1)}), bf16[128,4096]{1,0:T(8,128)(2,1)}) %all-gather.3.cloned.1.call-update) | async-done | bytes 1048592 | tf_op jit(solution)/shard_map/while/body/eval_jaxpr/all_gather | solution.py:73
  1421.2 3.3 add_convert_fusion.5
  1426.8 58.4 %psum.31 = f32[128,2,32]{0,2,1:T(8,128)S(1)} all-reduce(f32[128,2,32]{0,2,1:T(8,128)S(1)} %convolution_bitcast_fusion.5), channel_id=1, replica_groups=mesh['section'=8,'tp'=16] {'tp'}, use_global_device_ids=true, to_apply=%region_2.2 | all-reduce | flops 8192 | bytes 65536 | tf_op jit(solution)/shard_map/while/body/eval_jaxpr/psum | solution.py:82
  1487.5 17.7 %collective-permute-start = (bf16[128,4096]{1,0:T(8,128)(2,1)}, bf16[128,4096]{1,0:T(8,128)(2,1)S(1)}, u32[]{:S(2)}, u32[]{:S(2)}) collective-permute-start(bf16[128,4096]{1,0:T(8,128)(2,1)} %get-tuple-element.465), channel_id=1, source_target_pairs={{16,0},{32,16},{48,32},{64,48},{80,64},{96,80},{112,96},{17,1},{33... | collective-permute-start | bytes 3145736 | tf_op jit(solution)/shard_map/while/body/eval_jaxpr/ppermute | solution.py:15
  1505.2 13.7 collective-permute-done
  1523.5 37.6 %all-gather.3.cloned.1.call-done = bf16[128,4096]{1,0:T(8,128)(2,1)} async-done(((bf16[128,256]{1,0:T(8,128)(2,1)}), bf16[128,4096]{1,0:T(8,128)(2,1)}) %all-gather.3.cloned.1.call-update) | async-done | bytes 1048592 | tf_op jit(solution)/shard_map/while/body/eval_jaxpr/all_gather | solution.py:73
  1561.2 3.3 add_convert_fusion.5
  1566.8 58.4 %psum.31 = f32[128,2,32]{0,2,1:T(8,128)S(1)} all-reduce(f32[128,2,32]{0,2,1:T(8,128)S(1)} %convolution_bitcast_fusion.5), channel_id=1, replica_groups=mesh['section'=8,'tp'=16] {'tp'}, use_global_device_ids=true, to_apply=%region_2.2 | all-reduce | flops 8192 | bytes 65536 | tf_op jit(solution)/shard_map/while/body/eval_jaxpr/psum | solution.py:82
  1627.8 28.1 %psum.28 = f32[2,32]{1,0:T(2,128)} all-reduce(f32[2,32]{1,0:T(2,128)S(1)} %convolution_bitcast_fusion.3), channel_id=1, replica_groups=mesh['section'=8,'tp'=16] {'section'}, use_global_device_ids=true, to_apply=%region_4.5 | all-reduce | flops 64 | bytes 512 | tf_op jit(solution)/shard_map/psum | solution.py:107
  (185 shorter events, 85.7 us)
Async XLA Ops:
  6.5 1620.9 %copy-start = (bf16[2,32,2048]{2,1,0:T(8,128)(2,1)S(1)}, bf16[2,32,2048]{2,1,0:T(8,128)(2,1)}, u32[]{:S(2)}) copy-start(bf16[2,32,2048]{2,1,0:T(8,128)(2,1)} %param.13) | copy-start | bytes 786436
  6.5 2.3 copy-start.2
  6.5 90.4 %all-reduce.2.cloned.1.call-start = ((), (), s32[]{:S(2)}) async-start(), calls=%async_computation | async-start | bytes 524288 | tf_op jit(solution)/shard_map/psum | solution.py:49
  8.8 89.2 %copy-start.3 = (bf16[2,256,32]{1,2,0:T(8,128)(2,1)S(1)}, bf16[2,256,32]{1,2,0:T(8,128)(2,1)}, u32[]{:S(2)}) copy-start(bf16[2,256,32]{1,2,0:T(8,128)(2,1)} %param.12) | copy-start | bytes 98308
  8.8 89.2 %copy-start.4 = (s32[4]{0:T(128)S(1)}, s32[4]{0:T(128)}, u32[]{:S(2)}) copy-start(s32[4]{0:T(128)} %param.15) | copy-start | bytes 52
  98.0 62.9 %all-gather.3.cloned.1.call-start = ((), (), s32[]{:S(2)}) async-start(), calls=%async_computation.1 | async-start | bytes 1114112 | tf_op jit(solution)/shard_map/while/body/eval_jaxpr/all_gather | solution.py:73
  98.0 17.6 %collective-permute-start = (bf16[128,4096]{1,0:T(8,128)(2,1)}, bf16[128,4096]{1,0:T(8,128)(2,1)S(1)}, u32[]{:S(2)}, u32[]{:S(2)}) collective-permute-start(bf16[128,4096]{1,0:T(8,128)(2,1)} %get-tuple-element.465), channel_id=1, source_target_pairs={{16,0},{32,16},{48,32},{64,48},{80,64},{96,80},{112,96},{17,1},{33... | collective-permute-start | bytes 3145736 | tf_op jit(solution)/shard_map/while/body/eval_jaxpr/ppermute | solution.py:15
  120.2 46.2 %copy-start.1 = (bf16[128,256]{1,0:T(8,128)(2,1)S(1)}, bf16[128,256]{1,0:T(8,128)(2,1)}, u32[]{:S(2)}) copy-start(bf16[128,256]{1,0:T(8,128)(2,1)} %add_convert_fusion.4) | copy-start | bytes 196612 | tf_op jit(solution)/shard_map/while
  120.2 106.9 %all-gather.5.cloned.1.call-start = ((), (), s32[]{:S(2)}) async-start(), calls=%async_computation.2 | async-start | bytes 1114112 | tf_op jit(solution)/shard_map/while/body/eval_jaxpr/all_gather | solution.py:77
  227.2 73.7 %all-gather.3.cloned.1.call-start = ((), (), s32[]{:S(2)}) async-start(), calls=%async_computation.1 | async-start | bytes 1114112 | tf_op jit(solution)/shard_map/while/body/eval_jaxpr/all_gather | solution.py:73
  227.2 31.4 %collective-permute-start = (bf16[128,4096]{1,0:T(8,128)(2,1)}, bf16[128,4096]{1,0:T(8,128)(2,1)S(1)}, u32[]{:S(2)}, u32[]{:S(2)}) collective-permute-start(bf16[128,4096]{1,0:T(8,128)(2,1)} %get-tuple-element.465), channel_id=1, source_target_pairs={{16,0},{32,16},{48,32},{64,48},{80,64},{96,80},{112,96},{17,1},{33... | collective-permute-start | bytes 3145736 | tf_op jit(solution)/shard_map/while/body/eval_jaxpr/ppermute | solution.py:15
  263.2 43.2 %copy-start.1 = (bf16[128,256]{1,0:T(8,128)(2,1)S(1)}, bf16[128,256]{1,0:T(8,128)(2,1)}, u32[]{:S(2)}) copy-start(bf16[128,256]{1,0:T(8,128)(2,1)} %add_convert_fusion.4) | copy-start | bytes 196612 | tf_op jit(solution)/shard_map/while
  263.3 103.9 %all-gather.5.cloned.1.call-start = ((), (), s32[]{:S(2)}) async-start(), calls=%async_computation.2 | async-start | bytes 1114112 | tf_op jit(solution)/shard_map/while/body/eval_jaxpr/all_gather | solution.py:77
  367.2 73.8 %all-gather.3.cloned.1.call-start = ((), (), s32[]{:S(2)}) async-start(), calls=%async_computation.1 | async-start | bytes 1114112 | tf_op jit(solution)/shard_map/while/body/eval_jaxpr/all_gather | solution.py:73
  367.3 31.4 %collective-permute-start = (bf16[128,4096]{1,0:T(8,128)(2,1)}, bf16[128,4096]{1,0:T(8,128)(2,1)S(1)}, u32[]{:S(2)}, u32[]{:S(2)}) collective-permute-start(bf16[128,4096]{1,0:T(8,128)(2,1)} %get-tuple-element.465), channel_id=1, source_target_pairs={{16,0},{32,16},{48,32},{64,48},{80,64},{96,80},{112,96},{17,1},{33... | collective-permute-start | bytes 3145736 | tf_op jit(solution)/shard_map/while/body/eval_jaxpr/ppermute | solution.py:15
  403.3 43.2 %copy-start.1 = (bf16[128,256]{1,0:T(8,128)(2,1)S(1)}, bf16[128,256]{1,0:T(8,128)(2,1)}, u32[]{:S(2)}) copy-start(bf16[128,256]{1,0:T(8,128)(2,1)} %add_convert_fusion.4) | copy-start | bytes 196612 | tf_op jit(solution)/shard_map/while
  403.3 103.9 %all-gather.5.cloned.1.call-start = ((), (), s32[]{:S(2)}) async-start(), calls=%async_computation.2 | async-start | bytes 1114112 | tf_op jit(solution)/shard_map/while/body/eval_jaxpr/all_gather | solution.py:77
  507.2 73.8 %all-gather.3.cloned.1.call-start = ((), (), s32[]{:S(2)}) async-start(), calls=%async_computation.1 | async-start | bytes 1114112 | tf_op jit(solution)/shard_map/while/body/eval_jaxpr/all_gather | solution.py:73
  507.3 31.4 %collective-permute-start = (bf16[128,4096]{1,0:T(8,128)(2,1)}, bf16[128,4096]{1,0:T(8,128)(2,1)S(1)}, u32[]{:S(2)}, u32[]{:S(2)}) collective-permute-start(bf16[128,4096]{1,0:T(8,128)(2,1)} %get-tuple-element.465), channel_id=1, source_target_pairs={{16,0},{32,16},{48,32},{64,48},{80,64},{96,80},{112,96},{17,1},{33... | collective-permute-start | bytes 3145736 | tf_op jit(solution)/shard_map/while/body/eval_jaxpr/ppermute | solution.py:15
  543.3 43.2 %copy-start.1 = (bf16[128,256]{1,0:T(8,128)(2,1)S(1)}, bf16[128,256]{1,0:T(8,128)(2,1)}, u32[]{:S(2)}) copy-start(bf16[128,256]{1,0:T(8,128)(2,1)} %add_convert_fusion.4) | copy-start | bytes 196612 | tf_op jit(solution)/shard_map/while
  543.3 103.9 %all-gather.5.cloned.1.call-start = ((), (), s32[]{:S(2)}) async-start(), calls=%async_computation.2 | async-start | bytes 1114112 | tf_op jit(solution)/shard_map/while/body/eval_jaxpr/all_gather | solution.py:77
  647.3 73.8 %all-gather.3.cloned.1.call-start = ((), (), s32[]{:S(2)}) async-start(), calls=%async_computation.1 | async-start | bytes 1114112 | tf_op jit(solution)/shard_map/while/body/eval_jaxpr/all_gather | solution.py:73
  647.3 31.4 %collective-permute-start = (bf16[128,4096]{1,0:T(8,128)(2,1)}, bf16[128,4096]{1,0:T(8,128)(2,1)S(1)}, u32[]{:S(2)}, u32[]{:S(2)}) collective-permute-start(bf16[128,4096]{1,0:T(8,128)(2,1)} %get-tuple-element.465), channel_id=1, source_target_pairs={{16,0},{32,16},{48,32},{64,48},{80,64},{96,80},{112,96},{17,1},{33... | collective-permute-start | bytes 3145736 | tf_op jit(solution)/shard_map/while/body/eval_jaxpr/ppermute | solution.py:15
  683.3 43.2 %copy-start.1 = (bf16[128,256]{1,0:T(8,128)(2,1)S(1)}, bf16[128,256]{1,0:T(8,128)(2,1)}, u32[]{:S(2)}) copy-start(bf16[128,256]{1,0:T(8,128)(2,1)} %add_convert_fusion.4) | copy-start | bytes 196612 | tf_op jit(solution)/shard_map/while
  683.3 103.9 %all-gather.5.cloned.1.call-start = ((), (), s32[]{:S(2)}) async-start(), calls=%async_computation.2 | async-start | bytes 1114112 | tf_op jit(solution)/shard_map/while/body/eval_jaxpr/all_gather | solution.py:77
  787.3 73.8 %all-gather.3.cloned.1.call-start = ((), (), s32[]{:S(2)}) async-start(), calls=%async_computation.1 | async-start | bytes 1114112 | tf_op jit(solution)/shard_map/while/body/eval_jaxpr/all_gather | solution.py:73
  787.3 31.4 %collective-permute-start = (bf16[128,4096]{1,0:T(8,128)(2,1)}, bf16[128,4096]{1,0:T(8,128)(2,1)S(1)}, u32[]{:S(2)}, u32[]{:S(2)}) collective-permute-start(bf16[128,4096]{1,0:T(8,128)(2,1)} %get-tuple-element.465), channel_id=1, source_target_pairs={{16,0},{32,16},{48,32},{64,48},{80,64},{96,80},{112,96},{17,1},{33... | collective-permute-start | bytes 3145736 | tf_op jit(solution)/shard_map/while/body/eval_jaxpr/ppermute | solution.py:15
  823.3 43.2 %copy-start.1 = (bf16[128,256]{1,0:T(8,128)(2,1)S(1)}, bf16[128,256]{1,0:T(8,128)(2,1)}, u32[]{:S(2)}) copy-start(bf16[128,256]{1,0:T(8,128)(2,1)} %add_convert_fusion.4) | copy-start | bytes 196612 | tf_op jit(solution)/shard_map/while
  823.4 103.9 %all-gather.5.cloned.1.call-start = ((), (), s32[]{:S(2)}) async-start(), calls=%async_computation.2 | async-start | bytes 1114112 | tf_op jit(solution)/shard_map/while/body/eval_jaxpr/all_gather | solution.py:77
  927.3 73.8 %all-gather.3.cloned.1.call-start = ((), (), s32[]{:S(2)}) async-start(), calls=%async_computation.1 | async-start | bytes 1114112 | tf_op jit(solution)/shard_map/while/body/eval_jaxpr/all_gather | solution.py:73
  927.4 31.4 %collective-permute-start = (bf16[128,4096]{1,0:T(8,128)(2,1)}, bf16[128,4096]{1,0:T(8,128)(2,1)S(1)}, u32[]{:S(2)}, u32[]{:S(2)}) collective-permute-start(bf16[128,4096]{1,0:T(8,128)(2,1)} %get-tuple-element.465), channel_id=1, source_target_pairs={{16,0},{32,16},{48,32},{64,48},{80,64},{96,80},{112,96},{17,1},{33... | collective-permute-start | bytes 3145736 | tf_op jit(solution)/shard_map/while/body/eval_jaxpr/ppermute | solution.py:15
  963.4 43.2 %copy-start.1 = (bf16[128,256]{1,0:T(8,128)(2,1)S(1)}, bf16[128,256]{1,0:T(8,128)(2,1)}, u32[]{:S(2)}) copy-start(bf16[128,256]{1,0:T(8,128)(2,1)} %add_convert_fusion.4) | copy-start | bytes 196612 | tf_op jit(solution)/shard_map/while
  963.4 103.9 %all-gather.5.cloned.1.call-start = ((), (), s32[]{:S(2)}) async-start(), calls=%async_computation.2 | async-start | bytes 1114112 | tf_op jit(solution)/shard_map/while/body/eval_jaxpr/all_gather | solution.py:77
  1067.3 73.8 %all-gather.3.cloned.1.call-start = ((), (), s32[]{:S(2)}) async-start(), calls=%async_computation.1 | async-start | bytes 1114112 | tf_op jit(solution)/shard_map/while/body/eval_jaxpr/all_gather | solution.py:73
  1067.4 31.4 %collective-permute-start = (bf16[128,4096]{1,0:T(8,128)(2,1)}, bf16[128,4096]{1,0:T(8,128)(2,1)S(1)}, u32[]{:S(2)}, u32[]{:S(2)}) collective-permute-start(bf16[128,4096]{1,0:T(8,128)(2,1)} %get-tuple-element.465), channel_id=1, source_target_pairs={{16,0},{32,16},{48,32},{64,48},{80,64},{96,80},{112,96},{17,1},{33... | collective-permute-start | bytes 3145736 | tf_op jit(solution)/shard_map/while/body/eval_jaxpr/ppermute | solution.py:15
  1103.4 43.2 %copy-start.1 = (bf16[128,256]{1,0:T(8,128)(2,1)S(1)}, bf16[128,256]{1,0:T(8,128)(2,1)}, u32[]{:S(2)}) copy-start(bf16[128,256]{1,0:T(8,128)(2,1)} %add_convert_fusion.4) | copy-start | bytes 196612 | tf_op jit(solution)/shard_map/while
  1103.4 103.9 %all-gather.5.cloned.1.call-start = ((), (), s32[]{:S(2)}) async-start(), calls=%async_computation.2 | async-start | bytes 1114112 | tf_op jit(solution)/shard_map/while/body/eval_jaxpr/all_gather | solution.py:77
  1207.4 73.8 %all-gather.3.cloned.1.call-start = ((), (), s32[]{:S(2)}) async-start(), calls=%async_computation.1 | async-start | bytes 1114112 | tf_op jit(solution)/shard_map/while/body/eval_jaxpr/all_gather | solution.py:73
  1207.4 31.4 %collective-permute-start = (bf16[128,4096]{1,0:T(8,128)(2,1)}, bf16[128,4096]{1,0:T(8,128)(2,1)S(1)}, u32[]{:S(2)}, u32[]{:S(2)}) collective-permute-start(bf16[128,4096]{1,0:T(8,128)(2,1)} %get-tuple-element.465), channel_id=1, source_target_pairs={{16,0},{32,16},{48,32},{64,48},{80,64},{96,80},{112,96},{17,1},{33... | collective-permute-start | bytes 3145736 | tf_op jit(solution)/shard_map/while/body/eval_jaxpr/ppermute | solution.py:15
  1243.4 43.2 %copy-start.1 = (bf16[128,256]{1,0:T(8,128)(2,1)S(1)}, bf16[128,256]{1,0:T(8,128)(2,1)}, u32[]{:S(2)}) copy-start(bf16[128,256]{1,0:T(8,128)(2,1)} %add_convert_fusion.4) | copy-start | bytes 196612 | tf_op jit(solution)/shard_map/while
  1243.4 103.9 %all-gather.5.cloned.1.call-start = ((), (), s32[]{:S(2)}) async-start(), calls=%async_computation.2 | async-start | bytes 1114112 | tf_op jit(solution)/shard_map/while/body/eval_jaxpr/all_gather | solution.py:77
  1347.4 73.8 %all-gather.3.cloned.1.call-start = ((), (), s32[]{:S(2)}) async-start(), calls=%async_computation.1 | async-start | bytes 1114112 | tf_op jit(solution)/shard_map/while/body/eval_jaxpr/all_gather | solution.py:73
  1347.4 31.4 %collective-permute-start = (bf16[128,4096]{1,0:T(8,128)(2,1)}, bf16[128,4096]{1,0:T(8,128)(2,1)S(1)}, u32[]{:S(2)}, u32[]{:S(2)}) collective-permute-start(bf16[128,4096]{1,0:T(8,128)(2,1)} %get-tuple-element.465), channel_id=1, source_target_pairs={{16,0},{32,16},{48,32},{64,48},{80,64},{96,80},{112,96},{17,1},{33... | collective-permute-start | bytes 3145736 | tf_op jit(solution)/shard_map/while/body/eval_jaxpr/ppermute | solution.py:15
  1383.4 43.2 %copy-start.1 = (bf16[128,256]{1,0:T(8,128)(2,1)S(1)}, bf16[128,256]{1,0:T(8,128)(2,1)}, u32[]{:S(2)}) copy-start(bf16[128,256]{1,0:T(8,128)(2,1)} %add_convert_fusion.4) | copy-start | bytes 196612 | tf_op jit(solution)/shard_map/while
  1383.5 103.9 %all-gather.5.cloned.1.call-start = ((), (), s32[]{:S(2)}) async-start(), calls=%async_computation.2 | async-start | bytes 1114112 | tf_op jit(solution)/shard_map/while/body/eval_jaxpr/all_gather | solution.py:77
  1487.4 73.8 %all-gather.3.cloned.1.call-start = ((), (), s32[]{:S(2)}) async-start(), calls=%async_computation.1 | async-start | bytes 1114112 | tf_op jit(solution)/shard_map/while/body/eval_jaxpr/all_gather | solution.py:73
  1487.5 31.4 %collective-permute-start = (bf16[128,4096]{1,0:T(8,128)(2,1)}, bf16[128,4096]{1,0:T(8,128)(2,1)S(1)}, u32[]{:S(2)}, u32[]{:S(2)}) collective-permute-start(bf16[128,4096]{1,0:T(8,128)(2,1)} %get-tuple-element.465), channel_id=1, source_target_pairs={{16,0},{32,16},{48,32},{64,48},{80,64},{96,80},{112,96},{17,1},{33... | collective-permute-start | bytes 3145736 | tf_op jit(solution)/shard_map/while/body/eval_jaxpr/ppermute | solution.py:15
  1523.5 43.2 %copy-start.1 = (bf16[128,256]{1,0:T(8,128)(2,1)S(1)}, bf16[128,256]{1,0:T(8,128)(2,1)}, u32[]{:S(2)}) copy-start(bf16[128,256]{1,0:T(8,128)(2,1)} %add_convert_fusion.4) | copy-start | bytes 196612 | tf_op jit(solution)/shard_map/while
  1523.5 103.9 %all-gather.5.cloned.1.call-start = ((), (), s32[]{:S(2)}) async-start(), calls=%async_computation.2 | async-start | bytes 1114112 | tf_op jit(solution)/shard_map/while/body/eval_jaxpr/all_gather | solution.py:77
Sparse Core Ops, SparseCore 0:
  10.5 86.3 all-reduce.1
  120.3 40.5 all-gather.2
  164.4 42.9 all-gather.4
  263.4 37.5 all-gather.2
  304.4 42.9 all-gather.4
  403.4 37.5 all-gather.2
  444.4 42.9 all-gather.4
  543.4 37.5 all-gather.2
  584.5 42.9 all-gather.4
  683.4 37.5 all-gather.2
  724.5 42.9 all-gather.4
  823.5 37.5 all-gather.2
  864.5 42.9 all-gather.4
  963.5 37.5 all-gather.2
  1004.5 42.9 all-gather.4
  1103.5 37.5 all-gather.2
  1144.6 42.9 all-gather.4
  1243.5 37.5 all-gather.2
  1284.6 42.9 all-gather.4
  1383.6 37.5 all-gather.2
  1424.6 42.9 all-gather.4
  1523.6 37.5 all-gather.2
  1564.6 42.9 all-gather.4
where the time goes:
time: 1660 us
  blocking collectives  671 us (40%)
  waiting for transfers between devices  657 us (40%)
  starting transfers between devices  182 us (11%)
  matrix products  95 us (6%)
  other arithmetic  26.3 us (2%)
  local copies, waits for them, and re-layouts  17.8 us (1%)
    psum x11, blocking collectives, tick(): lax.psum(partial_out.reshape(block_rows, -1), 'tp')  643 us
    all_gather x11, waiting for transfers between devices, tick(): lax.all_gather(middle_own, 'tp', axis=1, tiled=True)  417 us
    ppermute x11, starting transfers between devices, from_behind(): return lax.ppermute(value, axis, pairs)  181 us
    ppermute x11, waiting for transfers between devices, from_behind(): return lax.ppermute(value, axis, pairs)  151 us
    psum x1, waiting for transfers between devices, shards(): lax.psum(partial_in.reshape(total_tokens, -1), 'tp')  87.7 us
    dot_general x11, matrix products, contract_columns(): lax.dot_general(portion, matrix, (((1,), (1,)), ((), ())), preferred_elem...  36.4 us
    dot_general x11, matrix products, tick(): lax.dot_general(upper_full, weights[1], (((1,), (1,)), ((), ())), preferr...  33.7 us
  transfers between devices with their start and end apart: 34, of which 23 were waited for; matrix products, arithmetic and copies ran while one was open for 3% of the time, Pallas kernels for 0%

commit v1 on v0

--- a/solution.py
+++ b/solution.py
@@ -70,7 +70,11 @@
         middle_own = (upper_own.astype(jnp.float32) + slope_block[1] * upper_branch).astype(
             jnp.bfloat16
         )
-        lower_branch = fold_lower(lax.all_gather(middle_own, "tp", axis=1, tiled=True))
+        lower_branch = fold_lower(
+            jnp.concatenate(
+                lax.all_to_all(jnp.stack([middle_own] * lax.axis_size("tp")), "tp", 0, 0), axis=1
+            )
+        )
         lower_own = (middle_own.astype(jnp.float32) + slope_block[0] * lower_branch).astype(
             jnp.bfloat16
         )

time: 1660 us -> 1380 us (0.83)
  waiting for transfers between devices: 657 us -> 388 us
  starting transfers between devices: 182 us -> 28.1 us
  blocking collectives: 671 us -> 810 us
    all_gather x11 -> x0, waiting for transfers between devices: 417 us -> none  [tick(): lax.all_gather(middle_own, 'tp', axis=1, tiled=True)]
    all_to_all x0 -> x11, blocking collectives: none -> 161 us  [tick(): lax.all_to_all(jnp.stack([middle_own] * lax.axis_size('tp')), 'tp', 0, 0)]
    ppermute x11, starting transfers between devices: 181 us -> 27.7 us  [from_behind(): return lax.ppermute(value, axis, pairs)]
    ppermute x11, waiting for transfers between devices: 151 us -> 299 us  [from_behind(): return lax.ppermute(value, axis, pairs)]
    psum x11, blocking collectives: 643 us -> 624 us  [tick(): lax.psum(partial_out.reshape(block_rows, -1), 'tp')]
  transfers between devices with their start and end apart: 34 -> 23, of which waited for: 23 -> 12; matrix products, arithmetic and copies ran while one was open for 3% -> 4% of each run, Pallas kernels for 0% -> 0%
where the time goes in v1:
time: 1380 us; the launch traced here: 1370 us
  blocking collectives  810 us (59%)
  waiting for transfers between devices  388 us (28%)
  matrix products  85.4 us (6%)
  starting transfers between devices  28.1 us (2%)
  other arithmetic  26.1 us (2%)
  local copies, waits for them, and re-layouts  21.2 us (2%)
    psum x11, blocking collectives, tick(): lax.psum(partial_out.reshape(block_rows, -1), 'tp')  624 us
    ppermute x11, waiting for transfers between devices, from_behind(): return lax.ppermute(value, axis, pairs)  299 us
    all_to_all x11, blocking collectives, tick(): lax.all_to_all(jnp.stack([middle_own] * lax.axis_size('tp')), 'tp', 0, 0)  161 us
    psum x1, waiting for transfers between devices, shards(): lax.psum(partial_in.reshape(total_tokens, -1), 'tp')  87.7 us
    dot_general x11, matrix products, contract_columns(): lax.dot_general(portion, matrix, (((1,), (1,)), ((), ())), preferred_elem...  33.7 us
    ppermute x11, starting transfers between devices, from_behind(): return lax.ppermute(value, axis, pairs)  27.7 us
  transfers between devices with their start and end apart: 23, of which 12 were waited for; matrix products, arithmetic and copies ran while one was open for 4% of the time, Pallas kernels for 0%

profile of v1, /device:TPU:1, one launch (start us, length us, event | category | flops | bytes accessed | tf_op | source)
XLA Modules:
  0.0 1372.8 jit_solution(4297888419931333008)
XLA Ops:
  6.5 2.2 convolution_bitcast_fusion.2
  9.2 87.7 %all-reduce.2.cloned.1.call-done = f32[512,2,64]{0,2,1:T(8,128)} async-done(((f32[512,2,64]{0,2,1:T(8,128)}), f32[512,2,64]{0,2,1:T(8,128)}) %all-reduce.2.cloned.1.call-update) | async-done | bytes 262160 | tf_op jit(solution)/shard_map/psum | solution.py:49
  98.0 1243.4 %while.18 = (s32[]{:T(128)}, bf16[128,4096]{1,0:T(8,128)(2,1)}, f32[2,2,2048]{2,1,0:T(2,128)S(1)}, pred[]{:T(512)}, s32[]{:T(128)}, /*index=5*/bf16[512,4096]{1,...) while((s32[]{:T(128)}, bf16[128,4096]{1,0:T(8,128)(2,1)}, ...), condition=%wide.region_3.4_spmd.clone, body=%wide.region_1.3_spmd.clone.sunk | while | flops 555048960 | bytes 25723832 | solution.py:105
  98.0 3.9 collective-permute-start
  101.9 13.7 %collective-permute-done = bf16[128,4096]{1,0:T(8,128)(2,1)S(1)} collective-permute-done((bf16[128,4096]{1,0:T(8,128)(2,1)}, bf16[128,4096]{1,0:T(8,128)(2,1)S(1)}, u32[]{:S(2)}, u32[]{:S(2)}) %collective-permute-start) | collective-permute-done | bytes 1048608 | tf_op jit(solution)/shard_map/while/body/eval_jaxpr/ppermute | solution.py:15
  117.1 2.4 add_convert_fusion.4
  119.9 16.3 %all_to_all.13 = bf16[16,128,256]{1,2,0:T(8,128)(2,1)S(1)} all-to-all(bf16[16,128,256]{1,2,0:T(8,128)(2,1)S(1)} %stack.53), channel_id=1, replica_groups=mesh['section'=8,'tp'=16] {'tp'}, dimensions={0} | all-to-all | bytes 2097152 | tf_op jit(solution)/shard_map/while/body/eval_jaxpr/all_to_all | solution.py:75
  136.2 3.1 add_convert_fusion.5
  141.6 56.6 %psum.31 = f32[128,2,32]{0,2,1:T(8,128)S(1)} all-reduce(f32[128,2,32]{0,2,1:T(8,128)S(1)} %convolution_bitcast_fusion.5), channel_id=1, replica_groups=mesh['section'=8,'tp'=16] {'tp'}, use_global_device_ids=true, to_apply=%region_2.2 | all-reduce | flops 8192 | bytes 65536 | tf_op jit(solution)/shard_map/while/body/eval_jaxpr/psum | solution.py:86
  200.4 6.5 collective-permute-start
  207.0 28.8 %collective-permute-done = bf16[128,4096]{1,0:T(8,128)(2,1)S(1)} collective-permute-done((bf16[128,4096]{1,0:T(8,128)(2,1)}, bf16[128,4096]{1,0:T(8,128)(2,1)S(1)}, u32[]{:S(2)}, u32[]{:S(2)}) %collective-permute-start) | collective-permute-done | bytes 1048608 | tf_op jit(solution)/shard_map/while/body/eval_jaxpr/ppermute | solution.py:15
  237.3 2.4 add_convert_fusion.4
  240.1 14.5 %all_to_all.13 = bf16[16,128,256]{1,2,0:T(8,128)(2,1)S(1)} all-to-all(bf16[16,128,256]{1,2,0:T(8,128)(2,1)S(1)} %stack.53), channel_id=1, replica_groups=mesh['section'=8,'tp'=16] {'tp'}, dimensions={0} | all-to-all | bytes 2097152 | tf_op jit(solution)/shard_map/while/body/eval_jaxpr/all_to_all | solution.py:75
  254.6 3.1 add_convert_fusion.5
  260.0 56.5 %psum.31 = f32[128,2,32]{0,2,1:T(8,128)S(1)} all-reduce(f32[128,2,32]{0,2,1:T(8,128)S(1)} %convolution_bitcast_fusion.5), channel_id=1, replica_groups=mesh['section'=8,'tp'=16] {'tp'}, use_global_device_ids=true, to_apply=%region_2.2 | all-reduce | flops 8192 | bytes 65536 | tf_op jit(solution)/shard_map/while/body/eval_jaxpr/psum | solution.py:86
  318.7 1.9 collective-permute-start
  320.6 32.6 %collective-permute-done = bf16[128,4096]{1,0:T(8,128)(2,1)S(1)} collective-permute-done((bf16[128,4096]{1,0:T(8,128)(2,1)}, bf16[128,4096]{1,0:T(8,128)(2,1)S(1)}, u32[]{:S(2)}, u32[]{:S(2)}) %collective-permute-start) | collective-permute-done | bytes 1048608 | tf_op jit(solution)/shard_map/while/body/eval_jaxpr/ppermute | solution.py:15
  354.7 2.4 add_convert_fusion.4
  357.4 14.6 %all_to_all.13 = bf16[16,128,256]{1,2,0:T(8,128)(2,1)S(1)} all-to-all(bf16[16,128,256]{1,2,0:T(8,128)(2,1)S(1)} %stack.53), channel_id=1, replica_groups=mesh['section'=8,'tp'=16] {'tp'}, dimensions={0} | all-to-all | bytes 2097152 | tf_op jit(solution)/shard_map/while/body/eval_jaxpr/all_to_all | solution.py:75
  372.0 3.1 add_convert_fusion.5
  377.4 56.6 %psum.31 = f32[128,2,32]{0,2,1:T(8,128)S(1)} all-reduce(f32[128,2,32]{0,2,1:T(8,128)S(1)} %convolution_bitcast_fusion.5), channel_id=1, replica_groups=mesh['section'=8,'tp'=16] {'tp'}, use_global_device_ids=true, to_apply=%region_2.2 | all-reduce | flops 8192 | bytes 65536 | tf_op jit(solution)/shard_map/while/body/eval_jaxpr/psum | solution.py:86
  436.2 1.9 collective-permute-start
  438.1 30.5 %collective-permute-done = bf16[128,4096]{1,0:T(8,128)(2,1)S(1)} collective-permute-done((bf16[128,4096]{1,0:T(8,128)(2,1)}, bf16[128,4096]{1,0:T(8,128)(2,1)S(1)}, u32[]{:S(2)}, u32[]{:S(2)}) %collective-permute-start) | collective-permute-done | bytes 1048608 | tf_op jit(solution)/shard_map/while/body/eval_jaxpr/ppermute | solution.py:15
  470.1 2.4 add_convert_fusion.4
  472.9 14.5 %all_to_all.13 = bf16[16,128,256]{1,2,0:T(8,128)(2,1)S(1)} all-to-all(bf16[16,128,256]{1,2,0:T(8,128)(2,1)S(1)} %stack.53), channel_id=1, replica_groups=mesh['section'=8,'tp'=16] {'tp'}, dimensions={0} | all-to-all | bytes 2097152 | tf_op jit(solution)/shard_map/while/body/eval_jaxpr/all_to_all | solution.py:75
  487.4 3.1 add_convert_fusion.5
  492.8 56.3 %psum.31 = f32[128,2,32]{0,2,1:T(8,128)S(1)} all-reduce(f32[128,2,32]{0,2,1:T(8,128)S(1)} %convolution_bitcast_fusion.5), channel_id=1, replica_groups=mesh['section'=8,'tp'=16] {'tp'}, use_global_device_ids=true, to_apply=%region_2.2 | all-reduce | flops 8192 | bytes 65536 | tf_op jit(solution)/shard_map/while/body/eval_jaxpr/psum | solution.py:86
  551.4 1.9 collective-permute-start
  553.3 28.1 %collective-permute-done = bf16[128,4096]{1,0:T(8,128)(2,1)S(1)} collective-permute-done((bf16[128,4096]{1,0:T(8,128)(2,1)}, bf16[128,4096]{1,0:T(8,128)(2,1)S(1)}, u32[]{:S(2)}, u32[]{:S(2)}) %collective-permute-start) | collective-permute-done | bytes 1048608 | tf_op jit(solution)/shard_map/while/body/eval_jaxpr/ppermute | solution.py:15
  582.9 2.4 add_convert_fusion.4
  585.7 14.5 %all_to_all.13 = bf16[16,128,256]{1,2,0:T(8,128)(2,1)S(1)} all-to-all(bf16[16,128,256]{1,2,0:T(8,128)(2,1)S(1)} %stack.53), channel_id=1, replica_groups=mesh['section'=8,'tp'=16] {'tp'}, dimensions={0} | all-to-all | bytes 2097152 | tf_op jit(solution)/shard_map/while/body/eval_jaxpr/all_to_all | solution.py:75
  600.1 3.1 add_convert_fusion.5
  605.5 56.9 %psum.31 = f32[128,2,32]{0,2,1:T(8,128)S(1)} all-reduce(f32[128,2,32]{0,2,1:T(8,128)S(1)} %convolution_bitcast_fusion.5), channel_id=1, replica_groups=mesh['section'=8,'tp'=16] {'tp'}, use_global_device_ids=true, to_apply=%region_2.2 | all-reduce | flops 8192 | bytes 65536 | tf_op jit(solution)/shard_map/while/body/eval_jaxpr/psum | solution.py:86
  666.6 27.6 %collective-permute-done = bf16[128,4096]{1,0:T(8,128)(2,1)S(1)} collective-permute-done((bf16[128,4096]{1,0:T(8,128)(2,1)}, bf16[128,4096]{1,0:T(8,128)(2,1)S(1)}, u32[]{:S(2)}, u32[]{:S(2)}) %collective-permute-start) | collective-permute-done | bytes 1048608 | tf_op jit(solution)/shard_map/while/body/eval_jaxpr/ppermute | solution.py:15
  695.7 2.4 add_convert_fusion.4
  698.4 14.5 %all_to_all.13 = bf16[16,128,256]{1,2,0:T(8,128)(2,1)S(1)} all-to-all(bf16[16,128,256]{1,2,0:T(8,128)(2,1)S(1)} %stack.53), channel_id=1, replica_groups=mesh['section'=8,'tp'=16] {'tp'}, dimensions={0} | all-to-all | bytes 2097152 | tf_op jit(solution)/shard_map/while/body/eval_jaxpr/all_to_all | solution.py:75
  712.9 3.1 add_convert_fusion.5
  718.3 56.9 %psum.31 = f32[128,2,32]{0,2,1:T(8,128)S(1)} all-reduce(f32[128,2,32]{0,2,1:T(8,128)S(1)} %convolution_bitcast_fusion.5), channel_id=1, replica_groups=mesh['section'=8,'tp'=16] {'tp'}, use_global_device_ids=true, to_apply=%region_2.2 | all-reduce | flops 8192 | bytes 65536 | tf_op jit(solution)/shard_map/while/body/eval_jaxpr/psum | solution.py:86
  779.4 27.6 %collective-permute-done = bf16[128,4096]{1,0:T(8,128)(2,1)S(1)} collective-permute-done((bf16[128,4096]{1,0:T(8,128)(2,1)}, bf16[128,4096]{1,0:T(8,128)(2,1)S(1)}, u32[]{:S(2)}, u32[]{:S(2)}) %collective-permute-start) | collective-permute-done | bytes 1048608 | tf_op jit(solution)/shard_map/while/body/eval_jaxpr/ppermute | solution.py:15
  808.4 2.4 add_convert_fusion.4
  811.2 14.5 %all_to_all.13 = bf16[16,128,256]{1,2,0:T(8,128)(2,1)S(1)} all-to-all(bf16[16,128,256]{1,2,0:T(8,128)(2,1)S(1)} %stack.53), channel_id=1, replica_groups=mesh['section'=8,'tp'=16] {'tp'}, dimensions={0} | all-to-all | bytes 2097152 | tf_op jit(solution)/shard_map/while/body/eval_jaxpr/all_to_all | solution.py:75
  825.7 3.1 add_convert_fusion.5
  831.1 56.9 %psum.31 = f32[128,2,32]{0,2,1:T(8,128)S(1)} all-reduce(f32[128,2,32]{0,2,1:T(8,128)S(1)} %convolution_bitcast_fusion.5), channel_id=1, replica_groups=mesh['section'=8,'tp'=16] {'tp'}, use_global_device_ids=true, to_apply=%region_2.2 | all-reduce | flops 8192 | bytes 65536 | tf_op jit(solution)/shard_map/while/body/eval_jaxpr/psum | solution.py:86
  892.2 27.6 %collective-permute-done = bf16[128,4096]{1,0:T(8,128)(2,1)S(1)} collective-permute-done((bf16[128,4096]{1,0:T(8,128)(2,1)}, bf16[128,4096]{1,0:T(8,128)(2,1)S(1)}, u32[]{:S(2)}, u32[]{:S(2)}) %collective-permute-start) | collective-permute-done | bytes 1048608 | tf_op jit(solution)/shard_map/while/body/eval_jaxpr/ppermute | solution.py:15
  921.3 2.4 add_convert_fusion.4
  924.0 14.5 %all_to_all.13 = bf16[16,128,256]{1,2,0:T(8,128)(2,1)S(1)} all-to-all(bf16[16,128,256]{1,2,0:T(8,128)(2,1)S(1)} %stack.53), channel_id=1, replica_groups=mesh['section'=8,'tp'=16] {'tp'}, dimensions={0} | all-to-all | bytes 2097152 | tf_op jit(solution)/shard_map/while/body/eval_jaxpr/all_to_all | solution.py:75
  938.5 3.1 add_convert_fusion.5
  943.9 56.9 %psum.31 = f32[128,2,32]{0,2,1:T(8,128)S(1)} all-reduce(f32[128,2,32]{0,2,1:T(8,128)S(1)} %convolution_bitcast_fusion.5), channel_id=1, replica_groups=mesh['section'=8,'tp'=16] {'tp'}, use_global_device_ids=true, to_apply=%region_2.2 | all-reduce | flops 8192 | bytes 65536 | tf_op jit(solution)/shard_map/while/body/eval_jaxpr/psum | solution.py:86
  1005.0 27.6 %collective-permute-done = bf16[128,4096]{1,0:T(8,128)(2,1)S(1)} collective-permute-done((bf16[128,4096]{1,0:T(8,128)(2,1)}, bf16[128,4096]{1,0:T(8,128)(2,1)S(1)}, u32[]{:S(2)}, u32[]{:S(2)}) %collective-permute-start) | collective-permute-done | bytes 1048608 | tf_op jit(solution)/shard_map/while/body/eval_jaxpr/ppermute | solution.py:15
  1034.1 2.4 add_convert_fusion.4
  1036.8 14.5 %all_to_all.13 = bf16[16,128,256]{1,2,0:T(8,128)(2,1)S(1)} all-to-all(bf16[16,128,256]{1,2,0:T(8,128)(2,1)S(1)} %stack.53), channel_id=1, replica_groups=mesh['section'=8,'tp'=16] {'tp'}, dimensions={0} | all-to-all | bytes 2097152 | tf_op jit(solution)/shard_map/while/body/eval_jaxpr/all_to_all | solution.py:75
  1051.3 3.1 add_convert_fusion.5
  1056.7 56.9 %psum.31 = f32[128,2,32]{0,2,1:T(8,128)S(1)} all-reduce(f32[128,2,32]{0,2,1:T(8,128)S(1)} %convolution_bitcast_fusion.5), channel_id=1, replica_groups=mesh['section'=8,'tp'=16] {'tp'}, use_global_device_ids=true, to_apply=%region_2.2 | all-reduce | flops 8192 | bytes 65536 | tf_op jit(solution)/shard_map/while/body/eval_jaxpr/psum | solution.py:86
  1117.8 27.6 %collective-permute-done = bf16[128,4096]{1,0:T(8,128)(2,1)S(1)} collective-permute-done((bf16[128,4096]{1,0:T(8,128)(2,1)}, bf16[128,4096]{1,0:T(8,128)(2,1)S(1)}, u32[]{:S(2)}, u32[]{:S(2)}) %collective-permute-start) | collective-permute-done | bytes 1048608 | tf_op jit(solution)/shard_map/while/body/eval_jaxpr/ppermute | solution.py:15
  1146.9 2.4 add_convert_fusion.4
  1149.6 14.5 %all_to_all.13 = bf16[16,128,256]{1,2,0:T(8,128)(2,1)S(1)} all-to-all(bf16[16,128,256]{1,2,0:T(8,128)(2,1)S(1)} %stack.53), channel_id=1, replica_groups=mesh['section'=8,'tp'=16] {'tp'}, dimensions={0} | all-to-all | bytes 2097152 | tf_op jit(solution)/shard_map/while/body/eval_jaxpr/all_to_all | solution.py:75
  1164.1 3.1 add_convert_fusion.5
  1169.5 56.9 %psum.31 = f32[128,2,32]{0,2,1:T(8,128)S(1)} all-reduce(f32[128,2,32]{0,2,1:T(8,128)S(1)} %convolution_bitcast_fusion.5), channel_id=1, replica_groups=mesh['section'=8,'tp'=16] {'tp'}, use_global_device_ids=true, to_apply=%region_2.2 | all-reduce | flops 8192 | bytes 65536 | tf_op jit(solution)/shard_map/while/body/eval_jaxpr/psum | solution.py:86
  1230.6 27.6 %collective-permute-done = bf16[128,4096]{1,0:T(8,128)(2,1)S(1)} collective-permute-done((bf16[128,4096]{1,0:T(8,128)(2,1)}, bf16[128,4096]{1,0:T(8,128)(2,1)S(1)}, u32[]{:S(2)}, u32[]{:S(2)}) %collective-permute-start) | collective-permute-done | bytes 1048608 | tf_op jit(solution)/shard_map/while/body/eval_jaxpr/ppermute | solution.py:15
  1259.7 2.4 add_convert_fusion.4
  1262.5 14.5 %all_to_all.13 = bf16[16,128,256]{1,2,0:T(8,128)(2,1)S(1)} all-to-all(bf16[16,128,256]{1,2,0:T(8,128)(2,1)S(1)} %stack.53), channel_id=1, replica_groups=mesh['section'=8,'tp'=16] {'tp'}, dimensions={0} | all-to-all | bytes 2097152 | tf_op jit(solution)/shard_map/while/body/eval_jaxpr/all_to_all | solution.py:75
  1276.9 3.1 add_convert_fusion.5
  1282.3 56.9 %psum.31 = f32[128,2,32]{0,2,1:T(8,128)S(1)} all-reduce(f32[128,2,32]{0,2,1:T(8,128)S(1)} %convolution_bitcast_fusion.5), channel_id=1, replica_groups=mesh['section'=8,'tp'=16] {'tp'}, use_global_device_ids=true, to_apply=%region_2.2 | all-reduce | flops 8192 | bytes 65536 | tf_op jit(solution)/shard_map/while/body/eval_jaxpr/psum | solution.py:86
  1341.7 24.2 %psum.28 = f32[2,32]{1,0:T(2,128)} all-reduce(f32[2,32]{1,0:T(2,128)S(1)} %convolution_bitcast_fusion.3), channel_id=1, replica_groups=mesh['section'=8,'tp'=16] {'section'}, use_global_device_ids=true, to_apply=%region_4.5 | all-reduce | flops 64 | bytes 512 | tf_op jit(solution)/shard_map/psum | solution.py:111
  (163 shorter events, 82.3 us)
Async XLA Ops:
  6.5 1334.9 %copy-start = (bf16[2,32,2048]{2,1,0:T(8,128)(2,1)S(1)}, bf16[2,32,2048]{2,1,0:T(8,128)(2,1)}, u32[]{:S(2)}) copy-start(bf16[2,32,2048]{2,1,0:T(8,128)(2,1)} %param.13) | copy-start | bytes 786436
  6.5 2.3 copy-start.1
  6.5 90.4 %all-reduce.2.cloned.1.call-start = ((), (), s32[]{:S(2)}) async-start(), calls=%async_computation.1 | async-start | bytes 524288 | tf_op jit(solution)/shard_map/psum | solution.py:49
  8.8 89.2 %copy-start.2 = (bf16[2,256,32]{1,2,0:T(8,128)(2,1)S(1)}, bf16[2,256,32]{1,2,0:T(8,128)(2,1)}, u32[]{:S(2)}) copy-start(bf16[2,256,32]{1,2,0:T(8,128)(2,1)} %param.12) | copy-start | bytes 98308
  8.8 89.2 %copy-start.3 = (s32[4]{0:T(128)S(1)}, s32[4]{0:T(128)}, u32[]{:S(2)}) copy-start(s32[4]{0:T(128)} %param.15) | copy-start | bytes 52
  98.0 102.4 %all-gather.2.cloned.1.call-start = ((), (), s32[]{:S(2)}) async-start(), calls=%async_computation.2 | async-start | bytes 1114112 | tf_op jit(solution)/shard_map/while/body/eval_jaxpr/all_gather | solution.py:81
  98.0 17.6 %collective-permute-start = (bf16[128,4096]{1,0:T(8,128)(2,1)}, bf16[128,4096]{1,0:T(8,128)(2,1)S(1)}, u32[]{:S(2)}, u32[]{:S(2)}) collective-permute-start(bf16[128,4096]{1,0:T(8,128)(2,1)} %get-tuple-element.465), channel_id=1, source_target_pairs={{16,0},{32,16},{48,32},{64,48},{80,64},{96,80},{112,96},{17,1},{33... | collective-permute-start | bytes 3145736 | tf_op jit(solution)/shard_map/while/body/eval_jaxpr/ppermute | solution.py:15
  200.4 118.2 %all-gather.2.cloned.1.call-start = ((), (), s32[]{:S(2)}) async-start(), calls=%async_computation.2 | async-start | bytes 1114112 | tf_op jit(solution)/shard_map/while/body/eval_jaxpr/all_gather | solution.py:81
  200.4 35.4 %collective-permute-start = (bf16[128,4096]{1,0:T(8,128)(2,1)}, bf16[128,4096]{1,0:T(8,128)(2,1)S(1)}, u32[]{:S(2)}, u32[]{:S(2)}) collective-permute-start(bf16[128,4096]{1,0:T(8,128)(2,1)} %get-tuple-element.465), channel_id=1, source_target_pairs={{16,0},{32,16},{48,32},{64,48},{80,64},{96,80},{112,96},{17,1},{33... | collective-permute-start | bytes 3145736 | tf_op jit(solution)/shard_map/while/body/eval_jaxpr/ppermute | solution.py:15
  318.6 117.5 %all-gather.2.cloned.1.call-start = ((), (), s32[]{:S(2)}) async-start(), calls=%async_computation.2 | async-start | bytes 1114112 | tf_op jit(solution)/shard_map/while/body/eval_jaxpr/all_gather | solution.py:81
  318.7 34.5 %collective-permute-start = (bf16[128,4096]{1,0:T(8,128)(2,1)}, bf16[128,4096]{1,0:T(8,128)(2,1)S(1)}, u32[]{:S(2)}, u32[]{:S(2)}) collective-permute-start(bf16[128,4096]{1,0:T(8,128)(2,1)} %get-tuple-element.465), channel_id=1, source_target_pairs={{16,0},{32,16},{48,32},{64,48},{80,64},{96,80},{112,96},{17,1},{33... | collective-permute-start | bytes 3145736 | tf_op jit(solution)/shard_map/while/body/eval_jaxpr/ppermute | solution.py:15
  436.1 115.2 %all-gather.2.cloned.1.call-start = ((), (), s32[]{:S(2)}) async-start(), calls=%async_computation.2 | async-start | bytes 1114112 | tf_op jit(solution)/shard_map/while/body/eval_jaxpr/all_gather | solution.py:81
  436.2 32.5 %collective-permute-start = (bf16[128,4096]{1,0:T(8,128)(2,1)}, bf16[128,4096]{1,0:T(8,128)(2,1)S(1)}, u32[]{:S(2)}, u32[]{:S(2)}) collective-permute-start(bf16[128,4096]{1,0:T(8,128)(2,1)} %get-tuple-element.465), channel_id=1, source_target_pairs={{16,0},{32,16},{48,32},{64,48},{80,64},{96,80},{112,96},{17,1},{33... | collective-permute-start | bytes 3145736 | tf_op jit(solution)/shard_map/while/body/eval_jaxpr/ppermute | solution.py:15
  551.3 113.2 %all-gather.2.cloned.1.call-start = ((), (), s32[]{:S(2)}) async-start(), calls=%async_computation.2 | async-start | bytes 1114112 | tf_op jit(solution)/shard_map/while/body/eval_jaxpr/all_gather | solution.py:81
  551.4 30.0 %collective-permute-start = (bf16[128,4096]{1,0:T(8,128)(2,1)}, bf16[128,4096]{1,0:T(8,128)(2,1)S(1)}, u32[]{:S(2)}, u32[]{:S(2)}) collective-permute-start(bf16[128,4096]{1,0:T(8,128)(2,1)} %get-tuple-element.465), channel_id=1, source_target_pairs={{16,0},{32,16},{48,32},{64,48},{80,64},{96,80},{112,96},{17,1},{33... | collective-permute-start | bytes 3145736 | tf_op jit(solution)/shard_map/while/body/eval_jaxpr/ppermute | solution.py:15
  664.6 112.8 %all-gather.2.cloned.1.call-start = ((), (), s32[]{:S(2)}) async-start(), calls=%async_computation.2 | async-start | bytes 1114112 | tf_op jit(solution)/shard_map/while/body/eval_jaxpr/all_gather | solution.py:81
  664.6 29.6 %collective-permute-start = (bf16[128,4096]{1,0:T(8,128)(2,1)}, bf16[128,4096]{1,0:T(8,128)(2,1)S(1)}, u32[]{:S(2)}, u32[]{:S(2)}) collective-permute-start(bf16[128,4096]{1,0:T(8,128)(2,1)} %get-tuple-element.465), channel_id=1, source_target_pairs={{16,0},{32,16},{48,32},{64,48},{80,64},{96,80},{112,96},{17,1},{33... | collective-permute-start | bytes 3145736 | tf_op jit(solution)/shard_map/while/body/eval_jaxpr/ppermute | solution.py:15
  777.4 112.7 %all-gather.2.cloned.1.call-start = ((), (), s32[]{:S(2)}) async-start(), calls=%async_computation.2 | async-start | bytes 1114112 | tf_op jit(solution)/shard_map/while/body/eval_jaxpr/all_gather | solution.py:81
  777.4 29.5 %collective-permute-start = (bf16[128,4096]{1,0:T(8,128)(2,1)}, bf16[128,4096]{1,0:T(8,128)(2,1)S(1)}, u32[]{:S(2)}, u32[]{:S(2)}) collective-permute-start(bf16[128,4096]{1,0:T(8,128)(2,1)} %get-tuple-element.465), channel_id=1, source_target_pairs={{16,0},{32,16},{48,32},{64,48},{80,64},{96,80},{112,96},{17,1},{33... | collective-permute-start | bytes 3145736 | tf_op jit(solution)/shard_map/while/body/eval_jaxpr/ppermute | solution.py:15
  890.2 112.8 %all-gather.2.cloned.1.call-start = ((), (), s32[]{:S(2)}) async-start(), calls=%async_computation.2 | async-start | bytes 1114112 | tf_op jit(solution)/shard_map/while/body/eval_jaxpr/all_gather | solution.py:81
  890.2 29.6 %collective-permute-start = (bf16[128,4096]{1,0:T(8,128)(2,1)}, bf16[128,4096]{1,0:T(8,128)(2,1)S(1)}, u32[]{:S(2)}, u32[]{:S(2)}) collective-permute-start(bf16[128,4096]{1,0:T(8,128)(2,1)} %get-tuple-element.465), channel_id=1, source_target_pairs={{16,0},{32,16},{48,32},{64,48},{80,64},{96,80},{112,96},{17,1},{33... | collective-permute-start | bytes 3145736 | tf_op jit(solution)/shard_map/while/body/eval_jaxpr/ppermute | solution.py:15
  1003.0 112.8 %all-gather.2.cloned.1.call-start = ((), (), s32[]{:S(2)}) async-start(), calls=%async_computation.2 | async-start | bytes 1114112 | tf_op jit(solution)/shard_map/while/body/eval_jaxpr/all_gather | solution.py:81
  1003.0 29.6 %collective-permute-start = (bf16[128,4096]{1,0:T(8,128)(2,1)}, bf16[128,4096]{1,0:T(8,128)(2,1)S(1)}, u32[]{:S(2)}, u32[]{:S(2)}) collective-permute-start(bf16[128,4096]{1,0:T(8,128)(2,1)} %get-tuple-element.465), channel_id=1, source_target_pairs={{16,0},{32,16},{48,32},{64,48},{80,64},{96,80},{112,96},{17,1},{33... | collective-permute-start | bytes 3145736 | tf_op jit(solution)/shard_map/while/body/eval_jaxpr/ppermute | solution.py:15
  1115.8 112.8 %all-gather.2.cloned.1.call-start = ((), (), s32[]{:S(2)}) async-start(), calls=%async_computation.2 | async-start | bytes 1114112 | tf_op jit(solution)/shard_map/while/body/eval_jaxpr/all_gather | solution.py:81
  1115.8 29.6 %collective-permute-start = (bf16[128,4096]{1,0:T(8,128)(2,1)}, bf16[128,4096]{1,0:T(8,128)(2,1)S(1)}, u32[]{:S(2)}, u32[]{:S(2)}) collective-permute-start(bf16[128,4096]{1,0:T(8,128)(2,1)} %get-tuple-element.465), channel_id=1, source_target_pairs={{16,0},{32,16},{48,32},{64,48},{80,64},{96,80},{112,96},{17,1},{33... | collective-permute-start | bytes 3145736 | tf_op jit(solution)/shard_map/while/body/eval_jaxpr/ppermute | solution.py:15
  1228.6 112.8 %all-gather.2.cloned.1.call-start = ((), (), s32[]{:S(2)}) async-start(), calls=%async_computation.2 | async-start | bytes 1114112 | tf_op jit(solution)/shard_map/while/body/eval_jaxpr/all_gather | solution.py:81
  1228.7 29.6 %collective-permute-start = (bf16[128,4096]{1,0:T(8,128)(2,1)}, bf16[128,4096]{1,0:T(8,128)(2,1)S(1)}, u32[]{:S(2)}, u32[]{:S(2)}) collective-permute-start(bf16[128,4096]{1,0:T(8,128)(2,1)} %get-tuple-element.465), channel_id=1, source_target_pairs={{16,0},{32,16},{48,32},{64,48},{80,64},{96,80},{112,96},{17,1},{33... | collective-permute-start | bytes 3145736 | tf_op jit(solution)/shard_map/while/body/eval_jaxpr/ppermute | solution.py:15
Sparse Core Ops, SparseCore 0:
  10.5 86.3 all-reduce.1
  139.4 45.5 all-gather.1
  257.8 42.4 all-gather.1
  375.2 39.9 all-gather.1
  490.6 37.3 all-gather.1
  603.3 37.3 all-gather.1
  716.1 37.3 all-gather.1
  828.9 37.3 all-gather.1
  941.7 37.4 all-gather.1
  1054.5 37.3 all-gather.1
  1167.3 37.3 all-gather.1
  1280.1 37.3 all-gather.1
